TPU v7x, 32 devices: a whole 2x2x4 slice. The times are simulated.
32 devices in a mesh: dp: 4 (over x, core), context: 2 (over y), tensor: 4 (over z).
Axes of the slice: x: 2, y: 2, z: 4, core: 2. Of those that a mesh axis runs over, the one named last changes fastest.
Arguments:
- layer_input: bfloat16 [4, 4096, 2048], P('dp', 'context'), may hold values from -6 to 6
- cotangent: bfloat16 [4, 4096, 2048], P('dp', 'context'), may hold values from -6 to 6
- w_qkv: bfloat16 [2048, 1536], P(('dp', 'context'), 'tensor'), may hold values from -0.125 to 0.125
- w_out: bfloat16 [1024, 2048], P('tensor', ('dp', 'context')), may hold values from -1.5 to 1.5
- attn_gain: bfloat16 [2048], P(('dp', 'context')), may hold values from 0.5 to 1.5
- qk_gain: float32 [2, 64], replicated, may hold values from 0.1 to 1.9
- w_gate: bfloat16 [2048, 5120], P(('dp', 'context'), 'tensor'), may hold values from -0.125 to 0.125
- w_up: bfloat16 [2048, 5120], P(('dp', 'context'), 'tensor'), may hold values from -0.125 to 0.125
- w_down: bfloat16 [5120, 2048], P('tensor', ('dp', 'context')), may hold values from -0.078125 to 0.078125
- ffn_gain: bfloat16 [2048], P(('dp', 'context')), may hold values from 0.5 to 1.5
- seg_ids: int32 [4, 4096], P('dp'), may hold values from 0 to 8, as said below
- pos_ids: int32 [4, 4096], P('dp'), may hold values from 0 to 2431, as said below
Outputs:
- layer_output: bfloat16 [4, 4096, 2048], P('dp', 'context')
- grad_input: bfloat16 [4, 4096, 2048], P('dp', 'context')
- grad_qkv: float32 [2048, 1536], P(('dp', 'context'), 'tensor')
- grad_out_proj: float32 [1024, 2048], P('tensor', ('dp', 'context'))
- grad_attn_gain: float32 [2048], P(('dp', 'context'))
- grad_qk_gain: float32 [2, 64], replicated
- grad_gate: float32 [2048, 5120], P(('dp', 'context'), 'tensor')
- grad_up: float32 [2048, 5120], P(('dp', 'context'), 'tensor')
- grad_down: float32 [5120, 2048], P('tensor', ('dp', 'context'))
- grad_ffn_gain: float32 [2048], P(('dp', 'context'))
Inputs may be any that keep to these rules, and one draw needn't show every extreme that they name: `seg_ids`: within each group the first 2048 tokens have id 0; the rest form 8 runs of consecutive tokens with ids 1 to 8 rising along the tokens, each run 1 to 384 tokens long, one of exactly 384 in every group. `pos_ids`: prompt token t has position t; the tokens of a continuation have positions 2048, 2049, ... in order.
All inputs are finite; a program needn't handle non-finite values.
Results may differ from a plain program's by a relative error of at most 0.024.
Values may be sent and summed in bfloat16 or wider, within the bound.
A program may use at most 256 MiB of HBM per device.

v0:
```python
import math
import jax
import jax.numpy as jnp
from jax import lax
from jax.sharding import PartitionSpec as P

HEADS = 16
KV_HEADS = 4
HEAD_DIM = 64
epsilon = 1e-06
rope_base = 10000.0


def norm_rows(values, gains):
    return values * lax.rsqrt(jnp.mean(values * values, axis=-1, keepdims=True) + epsilon) * gains


def rope_tables(positions, head_width):
    half_width = head_width // 2
    inverse = jnp.exp(
        -math.log(rope_base) * jnp.arange(half_width, dtype=jnp.float32) * 2.0 / head_width
    )
    angles = positions.astype(jnp.float32)[..., None] * inverse
    cosine_tab = jnp.concatenate([jnp.cos(angles), jnp.cos(angles)], axis=-1)
    sine_table = jnp.concatenate([jnp.sin(angles), jnp.sin(angles)], axis=-1)
    return (cosine_tab, sine_table)


def rotate(values, cosine_tab, sine_table):
    half_width = values.shape[-1] // 2
    lower_half = values[..., :half_width]
    upper_half = values[..., half_width:]
    return values * cosine_tab + jnp.concatenate([-upper_half, lower_half], axis=-1) * sine_table


def visible(query_pos, query_seg, key_pos, key_seg):
    same_run = (key_seg[None, :] == 0) | (key_seg[None, :] == query_seg[:, None])
    return (key_pos[None, :] <= query_pos[:, None]) & same_run


def mixed_silu(gate_in, up_in):
    return jax.nn.silu(gate_in) * up_in


def tensor_total(partial_term):
    return lax.psum(partial_term.astype(jnp.bfloat16), "tensor").astype(jnp.float32)


def body(
    layer_input,
    cotangent,
    w_qkv,
    w_out,
    attn_gain,
    qk_gain,
    w_gate,
    w_up,
    w_down,
    ffn_gain,
    seg_ids,
    pos_ids,
):
    group_count, local_len, model_width = layer_input.shape
    group_len = seg_ids.shape[1]
    kv_local = KV_HEADS // lax.axis_size("tensor")
    head_ratio = HEADS // KV_HEADS
    row_count = group_count * local_len
    score_scale = HEAD_DIM ** (-0.5)
    block_rows = min(local_len, 128)
    block_count = local_len // block_rows
    first_row = lax.axis_index("context") * local_len
    my_seg = lax.dynamic_slice_in_dim(seg_ids, first_row, local_len, 1)
    my_pos = lax.dynamic_slice_in_dim(pos_ids, first_row, local_len, 1)
    qkv_all, out_all, attn_gain_all = (
        lax.all_gather(w_qkv, ("dp", "context"), axis=0, tiled=True),
        lax.all_gather(w_out, ("dp", "context"), axis=1, tiled=True),
        lax.all_gather(attn_gain, ("dp", "context"), axis=0, tiled=True),
    )
    inputs = layer_input.astype(jnp.float32).reshape(row_count, model_width)
    normed = norm_rows(inputs, attn_gain_all.astype(jnp.float32))
    normed_low = normed.astype(jnp.bfloat16)
    joint = jnp.dot(normed_low, qkv_all, preferred_element_type=jnp.float32)
    joint = joint.reshape(group_count, local_len, kv_local, head_ratio + 2, HEAD_DIM)
    cosine_tab, sine_table = rope_tables(my_pos, HEAD_DIM)

    def prepare(query_raw, key_raw, gains_qk):
        query_rot = rotate(
            norm_rows(query_raw, gains_qk[0]),
            cosine_tab[:, :, None, None, :],
            sine_table[:, :, None, None, :],
        )
        key_rot = rotate(
            norm_rows(key_raw, gains_qk[1]), cosine_tab[:, :, None, :], sine_table[:, :, None, :]
        )
        return (query_rot, key_rot)

    query_raw = joint[:, :, :, :head_ratio]
    key_raw = joint[:, :, :, head_ratio]
    query_rot, key_rot = prepare(query_raw, key_raw, qk_gain)
    queries = query_rot.astype(jnp.bfloat16)
    kv_mine = jnp.stack([key_rot, joint[:, :, :, head_ratio + 1]], axis=3).astype(jnp.bfloat16)
    kv_mine = kv_mine.reshape(group_count, local_len, kv_local * 2 * HEAD_DIM)
    kv_group = lax.all_gather(kv_mine, "context", axis=1, tiled=True).reshape(
        group_count, group_len, kv_local, 2, HEAD_DIM
    )

    def block_scores(query_block, keys, allowed):
        scores = jnp.einsum("qkrd,tkd->qkrt", query_block, keys, preferred_element_type=jnp.float32)
        return jnp.where(allowed[:, None, None, :], scores * score_scale, -1e30)

    member = 0
    keys = kv_group[member, :, :, 0]
    values = kv_group[member, :, :, 1]
    key_pos = pos_ids[member]
    key_seg = seg_ids[member]

    def forward_block(block_items):
        query_block, query_pos, query_seg = block_items
        scores = block_scores(query_block, keys, visible(query_pos, query_seg, key_pos, key_seg))
        row_max = jnp.max(scores, axis=-1, keepdims=True)
        exp_scores = jnp.exp(scores - row_max)
        totals = jnp.sum(exp_scores, axis=-1, keepdims=True)
        probs = (exp_scores / totals).astype(jnp.bfloat16)
        result = jnp.einsum("qkrt,tkd->qkrd", probs, values, preferred_element_type=jnp.float32)
        return (result, row_max[..., 0] + jnp.log(totals[..., 0]))

    result, log_total = lax.map(
        forward_block,
        (
            queries[member].reshape(block_count, block_rows, kv_local, head_ratio, HEAD_DIM),
            my_pos[member].reshape(block_count, block_rows),
            my_seg[member].reshape(block_count, block_rows),
        ),
    )
    attended_list = [result]
    log_total_list = [log_total]
    attended_low = (
        jnp.stack(attended_list)
        .astype(jnp.bfloat16)
        .reshape(row_count, kv_local * head_ratio * HEAD_DIM)
    )
    attn_part = jnp.dot(attended_low, out_all, preferred_element_type=jnp.float32)
    gate_all, up_all, down_all, ffn_gain_all = (
        lax.all_gather(w_gate, ("dp", "context"), axis=0, tiled=True),
        lax.all_gather(w_up, ("dp", "context"), axis=0, tiled=True),
        lax.all_gather(w_down, ("dp", "context"), axis=1, tiled=True),
        lax.all_gather(ffn_gain, ("dp", "context"), axis=0, tiled=True),
    )
    resid = inputs + tensor_total(attn_part)
    normed_ffn_low = norm_rows(resid, ffn_gain_all.astype(jnp.float32)).astype(jnp.bfloat16)
    gate = jnp.dot(normed_ffn_low, gate_all, preferred_element_type=jnp.float32)
    up = jnp.dot(normed_ffn_low, up_all, preferred_element_type=jnp.float32)
    act_low = mixed_silu(gate, up).astype(jnp.bfloat16)
    ffn_part = jnp.dot(act_low, down_all, preferred_element_type=jnp.float32)
    result_out = (resid + tensor_total(ffn_part)).astype(jnp.bfloat16)
    gate_all, up_all, down_all, ffn_gain_all = (
        lax.all_gather(w_gate, ("dp", "context"), axis=0, tiled=True),
        lax.all_gather(w_up, ("dp", "context"), axis=0, tiled=True),
        lax.all_gather(w_down, ("dp", "context"), axis=1, tiled=True),
        lax.all_gather(ffn_gain, ("dp", "context"), axis=0, tiled=True),
    )
    qkv_all, out_all, attn_gain_all = (
        lax.all_gather(w_qkv, ("dp", "context"), axis=0, tiled=True),
        lax.all_gather(w_out, ("dp", "context"), axis=1, tiled=True),
        lax.all_gather(attn_gain, ("dp", "context"), axis=0, tiled=True),
    )
    cot_low = cotangent.reshape(row_count, model_width)
    grad_down = jnp.dot(act_low.T, cot_low, preferred_element_type=jnp.float32)
    act_grad = jnp.dot(cot_low, down_all.T, preferred_element_type=jnp.float32)
    _, silu_pull = jax.vjp(mixed_silu, gate, up)
    gate_grad, up_grad = silu_pull(act_grad)
    gate_grad = gate_grad.astype(jnp.bfloat16)
    up_grad = up_grad.astype(jnp.bfloat16)
    grad_gate = jnp.dot(normed_ffn_low.T, gate_grad, preferred_element_type=jnp.float32)
    grad_up = jnp.dot(normed_ffn_low.T, up_grad, preferred_element_type=jnp.float32)
    ffn_in_part = jnp.dot(gate_grad, gate_all.T, preferred_element_type=jnp.float32) + jnp.dot(
        up_grad, up_all.T, preferred_element_type=jnp.float32
    )
    ffn_in_grad = tensor_total(ffn_in_part)
    _, norm_ffn_pull = jax.vjp(norm_rows, resid, ffn_gain_all.astype(jnp.float32))
    resid_norm_grad, grad_ffn_gain = norm_ffn_pull(ffn_in_grad)
    resid_grad = cot_low.astype(jnp.float32) + resid_norm_grad
    branch_grad = resid_grad.astype(jnp.bfloat16)
    grad_out_proj = jnp.dot(attended_low.T, branch_grad, preferred_element_type=jnp.float32)
    attended_grad = jnp.dot(branch_grad, out_all.T, preferred_element_type=jnp.float32).astype(
        jnp.bfloat16
    )
    attended_grad = attended_grad.reshape(group_count, local_len, kv_local, head_ratio, HEAD_DIM)
    member = 0
    keys = kv_group[member, :, :, 0]
    values = kv_group[member, :, :, 1]
    key_pos = pos_ids[member]
    key_seg = seg_ids[member]

    def backward_block(carried, block_items):
        query_block, query_pos, query_seg, log_total, grad_block = block_items
        scores = block_scores(query_block, keys, visible(query_pos, query_seg, key_pos, key_seg))
        probs = jnp.exp(scores - log_total[..., None])
        prob_grad = jnp.einsum(
            "qkrd,tkd->qkrt", grad_block, values, preferred_element_type=jnp.float32
        )
        inner = jnp.sum(probs * prob_grad, axis=-1, keepdims=True)
        score_grad = (probs * (prob_grad - inner) * score_scale).astype(jnp.bfloat16)
        query_grad = jnp.einsum(
            "qkrt,tkd->qkrd", score_grad, keys, preferred_element_type=jnp.float32
        )
        key_total = carried[0] + jnp.einsum(
            "qkrt,qkrd->tkd", score_grad, query_block, preferred_element_type=jnp.float32
        )
        value_total = carried[1] + jnp.einsum(
            "qkrt,qkrd->tkd",
            probs.astype(jnp.bfloat16),
            grad_block,
            preferred_element_type=jnp.float32,
        )
        return ((key_total, value_total), query_grad)

    empty = jnp.zeros((group_len, kv_local, HEAD_DIM), jnp.float32)
    (key_total, value_total), query_grad = lax.scan(
        backward_block,
        (empty, empty),
        (
            queries[member].reshape(block_count, block_rows, kv_local, head_ratio, HEAD_DIM),
            my_pos[member].reshape(block_count, block_rows),
            my_seg[member].reshape(block_count, block_rows),
            log_total_list[member],
            attended_grad[member].reshape(block_count, block_rows, kv_local, head_ratio, HEAD_DIM),
        ),
    )
    query_grads = [query_grad.reshape(local_len, kv_local, head_ratio, HEAD_DIM)]
    key_grads = [key_total]
    value_grads = [value_total]
    kv_grad_group = jnp.stack([jnp.stack(key_grads), jnp.stack(value_grads)], axis=3)
    kv_grad_group = kv_grad_group.reshape(group_count, group_len, kv_local * 2 * HEAD_DIM)
    kv_grad = lax.psum_scatter(
        kv_grad_group.astype(jnp.bfloat16), "context", scatter_dimension=1, tiled=True
    ).astype(jnp.float32)
    kv_grad = kv_grad.reshape(group_count, local_len, kv_local, 2, HEAD_DIM)
    _, prepare_pull = jax.vjp(prepare, query_raw, key_raw, qk_gain)
    query_raw_grad, key_raw_grad, qk_gain_part = prepare_pull(
        (jnp.stack(query_grads), kv_grad[:, :, :, 0])
    )
    joint_grad = jnp.concatenate(
        [query_raw_grad, key_raw_grad[:, :, :, None], kv_grad[:, :, :, 1][:, :, :, None]], axis=3
    )
    joint_grad = joint_grad.astype(jnp.bfloat16).reshape(
        row_count, kv_local * (head_ratio + 2) * HEAD_DIM
    )
    grad_qkv = jnp.dot(normed_low.T, joint_grad, preferred_element_type=jnp.float32)
    in_part = jnp.dot(joint_grad, qkv_all.T, preferred_element_type=jnp.float32)
    in_grad = tensor_total(in_part)
    _, norm_in_pull = jax.vjp(norm_rows, inputs, attn_gain_all.astype(jnp.float32))
    input_norm_grad, grad_attn_gain = norm_in_pull(in_grad)
    grad_input = (resid_grad + input_norm_grad).astype(jnp.bfloat16)
    grad_input = grad_input.reshape(group_count, local_len, model_width)
    grad_qk_gain = lax.psum(qk_gain_part, ("dp", "context", "tensor"))
    grads = (grad_qkv, grad_out_proj, grad_attn_gain, grad_gate, grad_up, grad_down, grad_ffn_gain)
    shard_qkv, shard_out, shard_attn_gain, shard_gate, shard_up, shard_down, shard_ffn_gain = (
        lax.psum_scatter(
            grads[0].astype(jnp.bfloat16), ("dp", "context"), scatter_dimension=0, tiled=True
        ).astype(jnp.float32),
        lax.psum_scatter(
            grads[1].astype(jnp.bfloat16), ("dp", "context"), scatter_dimension=1, tiled=True
        ).astype(jnp.float32),
        lax.psum_scatter(
            grads[2].astype(jnp.bfloat16), ("dp", "context"), scatter_dimension=0, tiled=True
        ).astype(jnp.float32),
        lax.psum_scatter(
            grads[3].astype(jnp.bfloat16), ("dp", "context"), scatter_dimension=0, tiled=True
        ).astype(jnp.float32),
        lax.psum_scatter(
            grads[4].astype(jnp.bfloat16), ("dp", "context"), scatter_dimension=0, tiled=True
        ).astype(jnp.float32),
        lax.psum_scatter(
            grads[5].astype(jnp.bfloat16), ("dp", "context"), scatter_dimension=1, tiled=True
        ).astype(jnp.float32),
        lax.psum_scatter(
            grads[6].astype(jnp.bfloat16), ("dp", "context"), scatter_dimension=0, tiled=True
        ).astype(jnp.float32),
    )
    return (
        result_out.reshape(group_count, local_len, model_width),
        grad_input,
        shard_qkv,
        shard_out,
        shard_attn_gain,
        grad_qk_gain,
        shard_gate,
        shard_up,
        shard_down,
        shard_ffn_gain,
    )


def solution(mesh):
    return jax.shard_map(
        body,
        mesh=mesh,
        in_specs=(
            P("dp", "context", None),
            P("dp", "context", None),
            P(("dp", "context"), "tensor"),
            P("tensor", ("dp", "context")),
            P(("dp", "context")),
            P(),
            P(("dp", "context"), "tensor"),
            P(("dp", "context"), "tensor"),
            P("tensor", ("dp", "context")),
            P(("dp", "context")),
            P("dp", None),
            P("dp", None),
        ),
        out_specs=(
            P("dp", "context", None),
            P("dp", "context", None),
            P(("dp", "context"), "tensor"),
            P("tensor", ("dp", "context")),
            P(("dp", "context")),
            P(),
            P(("dp", "context"), "tensor"),
            P(("dp", "context"), "tensor"),
            P("tensor", ("dp", "context")),
            P(("dp", "context")),
        ),
        check_vma=False,
    )
```

profile of v0, /device:TPU:0, one launch (start us, length us, event | category | flops | bytes accessed | tf_op | source)
XLA Modules:
  0.0 2420.3 jit_solution(337184587082190026)
XLA Ops:
  8.6 14.2 all-gather
  31.0 7.3 all-gather.9.cloned.1.call-done
  40.9 6.5 fusion.85
  54.2 16.8 all-gather.11.cloned.1.call-done
  72.2 110.1 %while.27 = (s32[]{:T(128)}, bf16[16,128,1,4,64]{1,4,3,2,0:T(8,128)(2,1)}, f32[16,128,1,4]{1,3,2,0:T(4,128)}, s32[1,4096]{1,0:T(1,128)S(1)}, s32[16,128]{1,0:T(8...) while((s32[]{:T(128)}, ...), condition=%wide.region_6.7_spmd, body=%wide.region_3.6_spmd.sunk | while | flops 555748864 | bytes 27536516 | solution.py:127
  185.7 7.4 convolution_convert_fusion.2
  195.1 13.0 all-gather.1
  208.1 276.0 %all-reduce.14.cloned.1.call-done = bf16[2048,2048]{1,0:T(8,128)(2,1)} async-done(((bf16[2048,2048]{1,0:T(8,128)(2,1)}), bf16[2048,2048]{1,0:T(8,128)(2,1)}) %all-reduce.14.cloned.1.call-update) | async-done | bytes 8388624 | tf_op jit(solution)/shard_map/psum | solution.py:46
  484.1 8.5 multiply_reduce_fusion
  492.6 11.6 multiply_convert_fusion
  504.2 21.8 all-gather.17.cloned.1.call-done
  526.0 16.5 fusion.132
  542.5 26.4 %all-gather.15.cloned.1.call-done = bf16[2048,1280]{1,0:T(8,128)(2,1)} async-done(((bf16[256,1280]{1,0:T(8,128)(2,1)}), bf16[2048,1280]{1,0:T(8,128)(2,1)}) %all-gather.15.cloned.1.call-update) | async-done | bytes 5242896 | tf_op jit(solution)/shard_map/all_gather | solution.py:144
  568.9 16.6 fusion.131
  585.5 27.3 %all-gather.19.cloned.1.call-done = bf16[1280,2048]{1,0:T(8,128)(2,1)} async-done(((bf16[1280,256]{1,0:T(8,128)(2,1)}), bf16[1280,2048]{1,0:T(8,128)(2,1)}) %all-gather.19.cloned.1.call-update) | async-done | bytes 5242896 | tf_op jit(solution)/shard_map/all_gather | solution.py:146
  612.8 23.4 multiply_convert_fusion.1
  636.2 18.0 fusion.133
  654.2 19.0 add_convert_fusion
  673.4 290.9 %all-reduce.16.cloned.1.call-done = bf16[2048,2048]{1,0:T(8,128)(2,1)} async-done(((bf16[2048,2048]{1,0:T(8,128)(2,1)}), bf16[2048,2048]{1,0:T(8,128)(2,1)}) %all-reduce.16.cloned.1.call-update) | async-done | bytes 8388624 | tf_op jit(solution)/shard_map/psum | solution.py:46
  964.3 12.6 fusion.59
  976.9 14.4 fusion.61
  1008.7 505.4 %while.28 = (s32[]{:T(128)}, f32[4096,1,64]{0,2,1:T(8,128)S(1)}, f32[4096,1,64]{0,2,1:T(8,128)}, f32[16,128,1,4,64]{1,0,4,3,2:T(8,128)}, bf16[16,128,1,4,64]{1,4...) while((s32[]{:T(128)}, f32[4096,1,64]{0,2,1:T(8,128)S(1)}, ...), condition=%wide.region_14.15_spmd.clone, body=%wide.region_12.14_spmd.clone.sunk | while | flops 1366298112 | bytes 104010976 | solution.py:219
  1013.0 6.2 fusion.195
  1019.2 8.0 fusion.196
  1044.4 6.2 fusion.195
  1050.6 8.0 fusion.196
  1076.0 6.2 fusion.195
  1082.2 8.0 fusion.196
  1107.6 6.2 fusion.195
  1113.8 8.0 fusion.196
  1139.2 6.2 fusion.195
  1145.4 8.0 fusion.196
  1170.9 6.2 fusion.195
  1177.1 8.0 fusion.196
  1202.4 6.2 fusion.195
  1208.6 8.0 fusion.196
  1240.2 8.0 fusion.196
  1271.8 8.0 fusion.196
  1303.4 8.0 fusion.196
  1328.8 6.2 fusion.195
  1335.0 8.0 fusion.196
  1360.3 6.2 fusion.195
  1366.5 8.0 fusion.196
  1398.1 8.0 fusion.196
  1429.7 8.0 fusion.196
  1455.0 6.2 fusion.195
  1461.2 8.0 fusion.196
  1486.6 6.2 fusion.195
  1492.8 8.0 fusion.196
  1516.6 16.8 fusion.78
  1533.5 16.8 convolution_convert_fusion.3
  1550.4 17.8 convolution_convert_fusion.4
  1575.9 9.3 fusion.94
  1593.0 9.8 fusion.88
  1603.1 17.1 convolution_convert_fusion.1
  1620.2 6.8 convolution_convert_fusion
  1631.2 25.0 %reduce-scatter.15.cloned.1.call-done = bf16[256,1280]{1,0:T(8,128)(2,1)} async-done(((bf16[2048,1280]{1,0:T(8,128)(2,1)}), bf16[256,1280]{1,0:T(8,128)(2,1)}) %reduce-scatter.15.cloned.1.call-update) | async-done | bytes 655376 | tf_op jit(solution)/shard_map/reduce_scatter | solution.py:271
  1658.4 58.0 %reduce-scatter.13.cloned.1.call-done = bf16[256,1280]{1,0:T(8,128)(2,1)} async-done(((bf16[2048,1280]{1,0:T(8,128)(2,1)}), bf16[256,1280]{1,0:T(8,128)(2,1)}) %reduce-scatter.13.cloned.1.call-update) | async-done | bytes 655376 | tf_op jit(solution)/shard_map/reduce_scatter | solution.py:268
  1718.7 37.0 %reduce-scatter.11.cloned.1.call-done = bf16[256,256]{1,0:T(8,128)(2,1)} async-done(((bf16[256,2048]{1,0:T(8,128)(2,1)}), bf16[256,256]{1,0:T(8,128)(2,1)}) %reduce-scatter.11.cloned.1.call-update) | async-done | bytes 131088 | tf_op jit(solution)/shard_map/reduce_scatter | solution.py:262
  1757.3 39.3 %psum.39 = f32[2,64]{1,0:T(2,128)} all-reduce(f32[2,64]{1,0:T(2,128)S(1)} %pad_add_fusion.1), channel_id=1, replica_groups=mesh['dp'=4,'context'=2,'tensor'=4] {'dp','context','tensor'}, use_global_device_ids=true, to_apply=%region_26.27 | all-reduce | flops 128 | bytes 1024 | tf_op jit(solution)/shard_map/psum | solution.py:256
  1799.6 564.3 %all-reduce.18.cloned.1.call-done = (bf16[2048,2048]{1,0:T(8,128)(2,1)}, bf16[2048,2048]{1,0:T(8,128)(2,1)}) async-done(((bf16[2048,2048]{1,0:T(8,128)(2,1)}, bf16[2048,2048]{1,0:T(8,128)(2,1)}), (bf16[2048,2048]{1,0:T(8,128)(2,1)}, bf16[2048,2048]{1,0:T(8,128)(2,1)})) %all-reduce.18.cloned.1.call-update) | async-done | bytes 16777232 | tf_op jit(solution)/shard_map/psum | solution.py:46
  2363.9 10.1 fusion.60
  2374.0 14.3 all-reduce.8
  2389.6 24.0 fusion.69
  (487 shorter events, 492.1 us)
Async XLA Ops:
  7.2 21.5 copy-start.22
  7.2 31.1 %all-gather.9.cloned.1.call-start = ((), (), s32[]{:S(2)}) async-start(), calls=%async_computation.6 | async-start | bytes 1769472 | tf_op jit(solution)/shard_map/all_gather | solution.py:75
  7.9 63.1 %all-gather.11.cloned.1.call-start = ((), (), s32[]{:S(2)}) async-start(), calls=%async_computation.7 | async-start | bytes 1572864 | tf_op jit(solution)/shard_map/all_gather | solution.py:103
  22.8 24.7 %copy-start.31 = (f32[8,1,256]{2,1,0:T(1,128)}, f32[8,1,256]{2,1,0:T(1,128)S(1)}, u32[]{:S(2)}) copy-start(f32[8,1,256]{2,1,0:T(1,128)S(1)} %convert_element_type.227) | copy-start | bytes 24580
  23.6 24.8 %copy-start.44 = (f32[64]{0:T(128)}, f32[64]{0:T(128)S(1)}, u32[]{:S(2)}) copy-start(f32[64]{0:T(128)S(1)} %get-tuple-element.335) | copy-start | bytes 772
  23.6 29.3 %copy-start.42 = (f32[64]{0:T(128)}, f32[64]{0:T(128)S(1)}, u32[]{:S(2)}) copy-start(f32[64]{0:T(128)S(1)} %get-tuple-element.336) | copy-start | bytes 772
  28.7 18.8 copy-start.33
  31.0 19.8 copy-start.17
  40.9 7.5 copy-start.19
  40.9 11.1 copy-start.11
  47.5 5.4 copy-start.4
  49.5 136.2 %all-gather.13.cloned.1.call-start = ((), (), s32[]{:S(2)}) async-start(), calls=%async_computation.8 | async-start | bytes 1179648 | tf_op jit(solution)/shard_map/all_gather | solution.py:76
  50.2 433.9 %all-reduce.14.cloned.1.call-start = ((), (), s32[]{:S(2)}) async-start(), calls=%async_computation.9 | async-start | bytes 16777216 | tf_op jit(solution)/shard_map/psum | solution.py:46
  183.3 9.8 copy-start.2
  183.3 9.8 copy-start.6
  183.3 9.8 copy-start.39
  183.3 9.8 copy-start.40
  185.6 7.5 copy-start.9
  193.2 332.8 %all-gather.17.cloned.1.call-start = ((), (), s32[]{:S(2)}) async-start(), calls=%async_computation.11 | async-start | bytes 5898240 | tf_op jit(solution)/shard_map/all_gather | solution.py:145
  193.8 375.1 %all-gather.15.cloned.1.call-start = ((), (), s32[]{:S(2)}) async-start(), calls=%async_computation.10 | async-start | bytes 5898240 | tf_op jit(solution)/shard_map/all_gather | solution.py:144
  194.3 418.5 %all-gather.19.cloned.1.call-start = ((), (), s32[]{:S(2)}) async-start(), calls=%async_computation.12 | async-start | bytes 5898240 | tf_op jit(solution)/shard_map/all_gather | solution.py:146
  195.1 769.2 %all-reduce.16.cloned.1.call-start = ((), (), s32[]{:S(2)}) async-start(), calls=%async_computation.13 | async-start | bytes 16777216 | tf_op jit(solution)/shard_map/psum | solution.py:46
  673.3 915.6 %reduce-scatter.7.cloned.1.call-start = ((), (), s32[]{:S(2)}) async-start(), calls=%async_computation.14 | async-start | bytes 1572864 | tf_op jit(solution)/shard_map/reduce_scatter | solution.py:235
  976.9 20.1 copy-start.20
  991.2 5.7 copy-start.1
  997.0 11.7 copy-start.3
  997.0 11.7 copy-start.7
  997.0 11.7 copy-start.12
  997.0 11.7 copy-start.23
  1013.0 6.2 copy-start
  1044.4 6.2 copy-start
  1076.0 6.2 copy-start
  1107.6 6.2 copy-start
  1139.2 6.2 copy-start
  1170.8 6.2 copy-start
  1202.4 6.2 copy-start
  1234.0 6.2 copy-start
  1265.6 6.2 copy-start
  1297.2 6.2 copy-start
  1328.8 6.2 copy-start
  1360.3 6.2 copy-start
  1391.9 6.2 copy-start
  1423.5 6.2 copy-start
  1455.0 6.2 copy-start
  1486.6 6.2 copy-start
  1516.5 112.4 %reduce-scatter.17.cloned.1.call-start = ((), (), s32[]{:S(2)}) async-start(), calls=%async_computation.19 | async-start | bytes 5898240 | tf_op jit(solution)/shard_map/reduce_scatter | solution.py:274
  1533.4 122.8 %reduce-scatter.15.cloned.1.call-start = ((), (), s32[]{:S(2)}) async-start(), calls=%async_computation.18 | async-start | bytes 5898240 | tf_op jit(solution)/shard_map/reduce_scatter | solution.py:271
  1550.3 166.1 %reduce-scatter.13.cloned.1.call-start = ((), (), s32[]{:S(2)}) async-start(), calls=%async_computation.17 | async-start | bytes 5898240 | tf_op jit(solution)/shard_map/reduce_scatter | solution.py:268
  1568.2 5.2 copy-start.5
  1568.2 5.2 copy-start.26
  1568.2 5.2 copy-start.43
  1568.2 187.5 %reduce-scatter.11.cloned.1.call-start = ((), (), s32[]{:S(2)}) async-start(), calls=%async_computation.16 | async-start | bytes 1179648 | tf_op jit(solution)/shard_map/reduce_scatter | solution.py:262
  1571.1 4.8 copy-start.10
  1585.2 7.1 copy-start.18
  1585.2 7.1 copy-start.30
  1585.2 7.1 copy-start.45
  1585.2 7.4 copy-start.38
  1585.3 7.8 copy-start.32
  1585.3 7.8 copy-start.34
  1585.3 212.6 %reduce-scatter.9.cloned.1.call-start = ((), (), s32[]{:S(2)}) async-start(), calls=%async_computation.15 | async-start | bytes 1769472 | tf_op jit(solution)/shard_map/reduce_scatter | solution.py:259
  1602.8 17.4 copy-start.24
  1602.8 761.0 %all-reduce.18.cloned.1.call-start = ((), (), s32[]{:S(2)}) async-start(), calls=%async_computation.20 | async-start | bytes 33554432 | tf_op jit(solution)/shard_map/psum | solution.py:46
  2363.9 10.1 copy-start.36
  2363.9 10.1 copy-start.41
  (14 other events, 26.6 us)
Sparse Core Ops, SparseCore 0:
  9.9 28.3 all-gather.8
  49.6 21.3 all-gather.10
  72.9 23.5 all-gather.12
  193.2 290.8 all-reduce.13
  485.8 40.1 all-gather.16
  527.7 41.1 all-gather.14
  570.7 42.0 all-gather.18
  673.4 290.8 all-reduce.15
  1516.6 19.3 reduce-scatter.6
  1539.6 56.5 reduce-scatter.16
  1599.6 56.5 reduce-scatter.14
  1659.8 56.5 reduce-scatter.12
  1719.6 36.0 reduce-scatter.10
  1758.8 39.0 reduce-scatter.8
  1800.9 562.8 all-reduce.17
where the time goes:
time: 2430 us; the launch traced here: 2420 us
  waiting for transfers between devices  1360 us (56%)
  matrix products  547 us (23%)
  other arithmetic  295 us (12%)
  local copies, waits for them, and re-layouts  124 us (5%)
  blocking collectives  80.7 us (3%)
    psum x3, waiting for transfers between devices, tensor_total(): lax.psum(partial_term.astype(jnp.bfloat16), 'tensor').astype(jnp.float32)  1130 us
    another operation x19, other arithmetic  129 us
    dot_general x32, matrix products, block_scores(): jnp.einsum('qkrd,tkd->qkrt', query_block, keys, preferred_element_type=jn...  128 us
    dot_general x16, matrix products, backward_block(): jnp.einsum('qkrt,qkrd->tkd', probs.astype(jnp.bfloat16), grad_block, pref...  87.3 us
    dynamic_update_slice x16, local copies, waits for them, and re-layouts, body(): lax.map(forward_block, (queries[member].reshape(block_count, block_rows,...  72.3 us
    reduce_scatter x1, waiting for transfers between devices, body(): lax.psum_scatter(grads[3].astype(jnp.bfloat16), ('dp', 'context'), scatte...  58 us
  transfers between devices with their start and end apart: 15, of which 12 were waited for; matrix products, arithmetic and copies ran while one was open for 12% of the time, Pallas kernels for 0%

commit v1 on v0

--- a/solution.py
+++ b/solution.py
@@ -11,6 +11,11 @@
 rope_base = 10000.0
 
 
+def gather_and_add(x, axis):
+    parts = lax.all_gather(x, axis)
+    return jnp.sum(parts, axis=0)
+
+
 def norm_rows(values, gains):
     return values * lax.rsqrt(jnp.mean(values * values, axis=-1, keepdims=True) + epsilon) * gains
 
@@ -43,7 +48,7 @@
 
 
 def tensor_total(partial_term):
-    return lax.psum(partial_term.astype(jnp.bfloat16), "tensor").astype(jnp.float32)
+    return gather_and_add(partial_term.astype(jnp.bfloat16), "tensor").astype(jnp.float32)
 
 
 def body(

time: 2430 us -> 3600 us (1.48)
  waiting for transfers between devices: 1360 us -> 2410 us
  other arithmetic: 295 us -> 350 us
    all_gather x0 -> x4, waiting for transfers between devices: none -> 2230 us  [gather_and_add(): parts = lax.all_gather(x, axis)]
    psum x3 -> x0, waiting for transfers between devices: 1130 us -> none  [tensor_total(): lax.psum(partial_term.astype(jnp.bfloat16), 'tensor').astype(jnp.float32)]
    reduce_sum x0 -> x4, other arithmetic: none -> 67.4 us  [gather_and_add(): return jnp.sum(parts, axis=0)]
    reduce_scatter x1, waiting for transfers between devices: 58 us -> 0.02 us  [body(): lax.psum_scatter(grads[3].astype(jnp.bfloat16), ('dp', 'context'), scatte...]
    reduce_scatter x1, waiting for transfers between devices: 0.02 us -> 58 us  [body(): lax.psum_scatter(grads[5].astype(jnp.bfloat16), ('dp', 'context'), scatte...]
  transfers between devices with their start and end apart: 15 -> 16, of which waited for: 12 -> 13; matrix products, arithmetic and copies ran while one was open for 12% -> 9% of each run, Pallas kernels for 0% -> 0%
where the time goes in v1:
time: 3600 us; the launch traced here: 3590 us
  waiting for transfers between devices  2410 us (67%)
  matrix products  580 us (16%)
  other arithmetic  350 us (10%)
  local copies, waits for them, and re-layouts  151 us (4%)
  blocking collectives  80.1 us (2%)
    all_gather x4, waiting for transfers between devices, gather_and_add(): parts = lax.all_gather(x, axis)  2230 us
    another operation x19, other arithmetic  129 us
    dot_general x32, matrix products, block_scores(): jnp.einsum('qkrd,tkd->qkrt', query_block, keys, preferred_element_type=jn...  128 us
    dot_general x16, matrix products, backward_block(): jnp.einsum('qkrt,qkrd->tkd', probs.astype(jnp.bfloat16), grad_block, pref...  87.3 us
  transfers between devices with their start and end apart: 16, of which 13 were waited for; matrix products, arithmetic and copies ran while one was open for 9% of the time, Pallas kernels for 0%

profile of v1, /device:TPU:0, one launch (start us, length us, event | category | flops | bytes accessed | tf_op | source)
XLA Modules:
  0.0 3594.0 jit_solution(18386826115833395185)
XLA Ops:
  8.6 14.2 all-gather.4
  31.0 7.3 all-gather.17.cloned.1.call-done
  40.9 6.5 fusion.89
  55.4 15.6 all-gather.19.cloned.1.call-done
  72.3 109.8 %while.27 = (s32[]{:T(128)}, bf16[16,128,1,4,64]{1,4,3,2,0:T(8,128)(2,1)}, f32[16,128,1,4]{1,3,2,0:T(4,128)}, s32[1,4096]{1,0:T(1,128)S(1)}, s32[16,128]{1,0:T(8...) while((s32[]{:T(128)}, ...), condition=%wide.region_6.7_spmd, body=%wide.region_3.6_spmd.sunk | while | flops 555748864 | bytes 27537524 | solution.py:132
  185.4 7.4 convolution_convert_fusion.2
  194.8 12.3 all-gather.5
  207.2 547.2 %all-gather.29.cloned.1.call-done = bf16[8192,2048]{1,0:T(8,128)(2,1)} async-done(((bf16[2048,2048]{1,0:T(8,128)(2,1)}), bf16[8192,2048]{1,0:T(8,128)(2,1)}) %all-gather.29.cloned.1.call-update) | async-done | bytes 33554448 | tf_op jit(solution)/shard_map/all_gather | solution.py:15
  754.4 17.4 reduce_sum.185
  771.8 8.5 multiply_reduce_fusion
  780.9 11.3 multiply_convert_fusion
  795.4 16.6 fusion.136
  812.0 26.3 all-gather.25.cloned.1.call-done
  838.3 16.5 fusion.137
  854.8 27.4 all-gather.27.cloned.1.call-done
  882.3 23.6 multiply_convert_fusion.1
  905.9 18.0 fusion.138
  923.9 17.0 add_convert_fusion
  941.4 561.1 %all-gather.33.cloned.1.call-done = bf16[8192,2048]{1,0:T(8,128)(2,1)} async-done(((bf16[2048,2048]{1,0:T(8,128)(2,1)}), bf16[8192,2048]{1,0:T(8,128)(2,1)}) %all-gather.33.cloned.1.call-update) | async-done | bytes 33554448 | tf_op jit(solution)/shard_map/all_gather | solution.py:15
  1502.4 16.5 reduce_sum.191
  1518.9 13.3 fusion.60
  1532.3 12.5 fusion.95
  1553.2 557.9 %while.28 = (s32[]{:T(128)}, f32[4096,1,64]{0,2,1:T(8,128)S(1)}, f32[4096,1,64]{0,2,1:T(8,128)}, f32[16,128,1,4,64]{1,0,4,3,2:T(8,128)}, bf16[16,128,1,4,64]{1,4...) while((s32[]{:T(128)}, f32[4096,1,64]{0,2,1:T(8,128)S(1)}, ...), condition=%wide.region_14.15_spmd.clone, body=%wide.region_12.14_spmd.clone.sunk | while | flops 1366298112 | bytes 120790224 | solution.py:224
  1563.7 8.0 fusion.201
  1592.2 6.2 fusion.200
  1598.4 8.0 fusion.201
  1633.3 8.0 fusion.201
  1661.9 6.2 fusion.200
  1668.1 8.0 fusion.201
  1703.0 8.0 fusion.201
  1731.7 6.2 fusion.200
  1737.9 8.0 fusion.201
  1766.6 6.2 fusion.200
  1772.8 8.0 fusion.201
  1801.5 6.2 fusion.200
  1807.7 8.0 fusion.201
  1842.6 8.0 fusion.201
  1877.4 8.0 fusion.201
  1906.1 6.2 fusion.200
  1912.3 8.0 fusion.201
  1947.2 8.0 fusion.201
  1982.0 8.0 fusion.201
  2016.9 8.0 fusion.201
  2051.7 8.0 fusion.201
  2080.4 6.2 fusion.200
  2086.6 8.0 fusion.201
  2113.6 17.0 convolution_convert_fusion.4
  2130.7 16.8 convolution_convert_fusion.3
  2147.5 17.6 fusion.86
  2165.2 16.8 convolution_convert_fusion.1
  2191.4 13.8 fusion.98
  2209.6 9.9 fusion.92
  2219.6 7.0 convolution_convert_fusion
  2230.8 21.6 reduce-scatter.15.cloned.1.call-done
  2254.6 58.0 %reduce-scatter.17.cloned.1.call-done = bf16[1280,256]{1,0:T(8,128)(2,1)} async-done(((bf16[1280,2048]{1,0:T(8,128)(2,1)}), bf16[1280,256]{1,0:T(8,128)(2,1)}) %reduce-scatter.17.cloned.1.call-update) | async-done | bytes 655376 | tf_op jit(solution)/shard_map/reduce_scatter | solution.py:279
  2314.8 560.8 %all-gather.31.cloned.1.call-done = bf16[8192,2048]{1,0:T(8,128)(2,1)} async-done(((bf16[2048,2048]{1,0:T(8,128)(2,1)}), bf16[8192,2048]{1,0:T(8,128)(2,1)}) %all-gather.31.cloned.1.call-update) | async-done | bytes 33554448 | tf_op jit(solution)/shard_map/all_gather | solution.py:15
  2875.6 17.0 reduce_sum.190
  2892.5 20.3 reduce-scatter.11.cloned.1.call-done
  2914.5 39.3 %psum.7 = f32[2,64]{1,0:T(2,128)} all-reduce(f32[2,64]{1,0:T(2,128)S(1)} %pad_add_fusion.1), channel_id=1, replica_groups=mesh['dp'=4,'context'=2,'tensor'=4] {'dp','context','tensor'}, use_global_device_ids=true, to_apply=%region_26.27 | all-reduce | flops 128 | bytes 1024 | tf_op jit(solution)/shard_map/psum | solution.py:261
  2956.8 561.4 %all-gather.35.cloned.1.call-done = bf16[8192,2048]{1,0:T(8,128)(2,1)} async-done(((bf16[2048,2048]{1,0:T(8,128)(2,1)}), bf16[8192,2048]{1,0:T(8,128)(2,1)}) %all-gather.35.cloned.1.call-update) | async-done | bytes 33554448 | tf_op jit(solution)/shard_map/all_gather | solution.py:15
  3518.2 16.6 reduce_sum.198
  3534.7 10.1 fusion.63
  3544.8 14.3 all-reduce.8
  3560.4 26.7 fusion.57
  (548 shorter events, 563.6 us)
Async XLA Ops:
  7.2 21.5 copy-start.22
  7.2 31.1 all-gather.17.cloned.1.call-start
  7.9 63.1 %all-gather.19.cloned.1.call-start = ((), (), s32[]{:S(2)}) async-start(), calls=%async_computation.7 | async-start | bytes 1572864 | tf_op jit(solution)/shard_map/all_gather | solution.py:108
  22.8 24.7 copy-start.36
  23.6 24.8 copy-start.53
  23.6 30.3 copy-start.51
  28.7 18.8 copy-start.38
  31.0 19.8 copy-start.18
  40.9 7.5 copy-start.20
  40.9 12.0 copy-start.10
  47.5 6.4 copy-start.5
  49.5 135.9 %all-gather.21.cloned.1.call-start = ((), (), s32[]{:S(2)}) async-start(), calls=%async_computation.8 | async-start | bytes 1179648 | tf_op jit(solution)/shard_map/all_gather | solution.py:81
  50.2 704.1 %all-gather.29.cloned.1.call-start = ((), (), s32[]{:S(2)}) async-start(), calls=%async_computation.18 | async-start | bytes 41943040 | tf_op jit(solution)/shard_map/all_gather | solution.py:15
  183.0 9.8 copy-start.2
  183.0 9.8 copy-start.7
  183.0 9.8 copy-start.48
  183.0 9.8 copy-start.49
  185.3 7.5 copy-start.12
  192.9 602.6 %all-gather.23.cloned.1.call-start = ((), (), s32[]{:S(2)}) async-start(), calls=%async_computation.9 | async-start | bytes 5898240 | tf_op jit(solution)/shard_map/all_gather | solution.py:149
  193.4 644.9 %all-gather.25.cloned.1.call-start = ((), (), s32[]{:S(2)}) async-start(), calls=%async_computation.10 | async-start | bytes 5898240 | tf_op jit(solution)/shard_map/all_gather | solution.py:150
  194.0 688.2 %all-gather.27.cloned.1.call-start = ((), (), s32[]{:S(2)}) async-start(), calls=%async_computation.11 | async-start | bytes 5898240 | tf_op jit(solution)/shard_map/all_gather | solution.py:151
  194.8 1307.7 %all-gather.33.cloned.1.call-start = ((), (), s32[]{:S(2)}) async-start(), calls=%async_computation.20 | async-start | bytes 41943040 | tf_op jit(solution)/shard_map/all_gather | solution.py:15
  207.2 1325.1 %copy-start.32 = (f32[8,1,256]{2,1,0:T(1,128)}, f32[8,1,256]{2,1,0:T(1,128)S(1)}, u32[]{:S(2)}) copy-start(f32[8,1,256]{2,1,0:T(1,128)S(1)} %convert_element_type.311) | copy-start | bytes 24580
  780.9 751.3 %copy-start.34 = (f32[2048]{0:T(1024)}, f32[2048]{0:T(1024)S(1)}, u32[]{:S(2)}) copy-start(f32[2048]{0:T(1024)S(1)} %fusion.131) | copy-start | bytes 24580
  905.9 18.0 copy-start.55
  940.9 1264.4 %reduce-scatter.7.cloned.1.call-start = ((), (), s32[]{:S(2)}) async-start(), calls=%async_computation.12 | async-start | bytes 1572864 | tf_op jit(solution)/shard_map/reduce_scatter | solution.py:240
  1518.9 13.3 copy-start.45
  1518.9 13.3 copy-start.4
  1518.9 13.3 copy-start.25
  1532.3 12.6 copy-start.46
  1532.3 20.9 copy-start.3
  1532.3 20.9 copy-start.8
  1532.3 20.9 copy-start.11
  1532.3 20.9 copy-start.23
  1556.8 6.9 copy-start
  1591.5 6.8 copy-start
  1626.4 6.9 copy-start
  1661.3 6.8 copy-start
  1696.1 6.8 copy-start
  1731.0 6.9 copy-start
  1765.9 6.9 copy-start
  1800.8 6.9 copy-start
  1835.7 6.9 copy-start
  1870.6 6.9 copy-start
  1905.4 6.9 copy-start
  1940.3 6.9 copy-start
  1975.1 6.8 copy-start
  2010.0 6.9 copy-start
  2044.9 6.8 copy-start
  2079.7 6.9 copy-start
  2113.6 115.0 %reduce-scatter.13.cloned.1.call-start = ((), (), s32[]{:S(2)}) async-start(), calls=%async_computation.15 | async-start | bytes 5898240 | tf_op jit(solution)/shard_map/reduce_scatter | solution.py:273
  2130.6 121.8 %reduce-scatter.15.cloned.1.call-start = ((), (), s32[]{:S(2)}) async-start(), calls=%async_computation.16 | async-start | bytes 5898240 | tf_op jit(solution)/shard_map/reduce_scatter | solution.py:276
  2147.5 165.1 %reduce-scatter.17.cloned.1.call-start = ((), (), s32[]{:S(2)}) async-start(), calls=%async_computation.17 | async-start | bytes 5898240 | tf_op jit(solution)/shard_map/reduce_scatter | solution.py:279
  2165.1 710.5 %all-gather.31.cloned.1.call-start = ((), (), s32[]{:S(2)}) async-start(), calls=%async_computation.19 | async-start | bytes 41943040 | tf_op jit(solution)/shard_map/all_gather | solution.py:15
  2182.0 730.9 %reduce-scatter.11.cloned.1.call-start = ((), (), s32[]{:S(2)}) async-start(), calls=%async_computation.14 | async-start | bytes 1179648 | tf_op jit(solution)/shard_map/reduce_scatter | solution.py:267
  2191.4 16.4 copy-start.19
  2191.4 16.4 copy-start.31
  2191.4 16.4 copy-start.54
  2191.4 16.7 copy-start.43
  2205.2 749.9 %reduce-scatter.9.cloned.1.call-start = ((), (), s32[]{:S(2)}) async-start(), calls=%async_computation.13 | async-start | bytes 1769472 | tf_op jit(solution)/shard_map/reduce_scatter | solution.py:264
  2209.5 10.0 copy-start.24
  2219.5 1298.6 %all-gather.35.cloned.1.call-start = ((), (), s32[]{:S(2)}) async-start(), calls=%async_computation.21 | async-start | bytes 41943040 | tf_op jit(solution)/shard_map/all_gather | solution.py:15
  3534.7 10.1 copy-start.50
  3534.7 25.7 copy-start.41
  (42 other events, 102.6 us)
Sparse Core Ops, SparseCore 0:
  9.9 28.3 all-gather.16
  49.6 21.3 all-gather.18
  72.9 23.5 all-gather.20
  192.9 561.3 all-gather.28
  756.1 39.2 all-gather.22
  797.2 41.1 all-gather.24
  840.2 42.0 all-gather.26
  941.0 561.3 all-gather.32
  2113.7 18.4 reduce-scatter.6
  2135.8 56.5 reduce-scatter.12
  2195.8 56.5 reduce-scatter.14
  2256.0 56.5 reduce-scatter.16
  2314.2 561.3 all-gather.30
  2878.6 34.2 reduce-scatter.10
  2916.0 39.0 reduce-scatter.8
  2957.1 561.0 all-gather.34
